TPU v7x, 32 devices: a whole 2x2x4 slice. The times are simulated.
32 devices in a mesh: tok: 4 (over y, x), col: 8 (over z, core).
Axes of the slice: x: 2, y: 2, z: 4, core: 2. Of those that a mesh axis runs over, the one named last changes fastest.
Arguments:
- activations: bfloat16 [8192, 8192], P('tok', 'col'), may hold values from -60 to 60, as said below
- weight: bfloat16 [8192, 8192], P('tok', 'col'), may hold values from -6 to 6
- keep_mask: int32 [8192, 8192], P('tok', 'col'), may hold values from 0 to 1
Outputs:
- new_weight: bfloat16 [8192, 8192], P('tok', 'col')
Inputs may be any that keep to these rules, and one draw needn't show every extreme that they name: activations of calibration tokens.
All inputs are finite; a program needn't handle non-finite values.
Results may differ from a plain program's by a relative error of at most 0.00115.
Values may be sent and summed in bfloat16 or wider, within the bound.
No kernel may reach another device: no remote copies, remote signals or barrier semaphores. Data moves between devices by JAX's collectives and lax.ppermute only.
A program may use at most 128 MiB of HBM per device.

v0:
```python
import jax
import jax.numpy as jnp
from jax import lax
from jax.sharding import PartitionSpec as P

B = 1024
ITERS = 4


def per_device(activations, weight, keep_mask):
    highest = lax.Precision.HIGHEST
    n_col = lax.axis_size("col")
    n_tok = lax.axis_size("tok")
    tok_rows = activations.shape[0]
    panel_width = B // n_col
    total_count = tok_rows * n_tok
    partial_panel = lax.dot_general(
        activations,
        lax.all_gather(activations[:, :panel_width], "col", axis=1, tiled=True),
        (((0,), (0,)), ((), ())),
        preferred_element_type=jnp.float32,
    )
    block_part = lax.psum(partial_panel[:panel_width], "tok") / total_count
    diagonal_block = lax.all_gather(block_part, "col", axis=0, tiled=True)
    identity = jnp.eye(B, dtype=jnp.float32)
    damping = 0.01 * jnp.mean(jnp.diagonal(diagonal_block))
    damped = diagonal_block + damping * identity
    frobenius = jnp.sqrt(jnp.sum(damped * damped))
    col_index = lax.axis_index("col")
    row_ids = col_index * panel_width + lax.iota(jnp.int32, panel_width)
    iterate = (row_ids[:, None] == lax.iota(jnp.int32, B)[None, :]).astype(jnp.float32) / frobenius
    for sweep in range(ITERS):
        if sweep == 0:
            whole = identity / frobenius
        else:
            whole = lax.all_gather(iterate.astype(jnp.bfloat16), "col", axis=0, tiled=True).astype(
                iterate.dtype
            )
        product = jnp.dot(iterate, damped, precision=highest)
        iterate = 2.0 * iterate - jnp.dot(product, whole, precision=highest)
    inverse = lax.all_gather(iterate, "col", axis=0, tiled=True)
    remainder = lax.psum(partial_panel[panel_width:], "tok") / total_count
    hessian_panel = jnp.concatenate([block_part, remainder], axis=0)
    pruned = jnp.where(
        keep_mask[:, :panel_width] == 0, weight[:, :panel_width], jnp.zeros((), jnp.bfloat16)
    )
    pruned_panel = lax.all_gather(pruned, "col", axis=1, tiled=True).astype(jnp.float32)
    factor_rows = jnp.dot(pruned_panel, inverse, precision=highest)
    correction = lax.dot_general(
        factor_rows, hessian_panel, (((1,), (1,)), ((), ())), precision=highest
    )
    kept = keep_mask.astype(jnp.float32)
    return (kept * (weight.astype(jnp.float32) - correction)).astype(jnp.bfloat16)


def solution(mesh):
    return jax.shard_map(
        per_device,
        mesh=mesh,
        in_specs=(P("tok", "col"), P("tok", "col"), P("tok", "col")),
        out_specs=P("tok", "col"),
        check_vma=False,
    )
```

profile of v0, /device:TPU:0, one launch (start us, length us, event | category | flops | bytes accessed | tf_op | source)
XLA Modules:
  0.0 493.3 jit_solution(1033233946870937970)
XLA Ops:
  6.5 0.0 all-gather.10.cloned.1.call-start
  6.5 1.9 slice.17
  8.4 0.0 all-gather.10.cloned.1.call-update
  8.4 0.0 all-reduce.3.cloned.1.call-start
  8.5 51.0 %all-gather.10.cloned.1.call-done = bf16[2048,1024]{1,0:T(8,128)(2,1)} async-done(((bf16[2048,128]{1,0:T(8,128)(2,1)}), bf16[2048,1024]{1,0:T(8,128)(2,1)}) %all-gather.10.cloned.1.call-update) | async-done | bytes 4194320 | tf_op jit(solution)/shard_map/all_gather | solution.py:19
  59.5 7.6 %fusion.31 = f32[1024,1024]{1,0:T(8,128)S(1)} fusion(bf16[2048,1024]{1,0:T(8,128)(2,1)} %param.3, bf16[2048,1024]{1,0:T(8,128)(2,1)} %all-gather.10.cloned.1.call-done), kind=kOutput, calls=%fused_computation.42 | convolution fusion | flops 4294967296 | bytes 12582912 | tf_op jit(solution)/shard_map/dot_general | solution.py:17
  67.1 0.8 slice.22
  67.9 2.3 slice.23
  70.2 0.0 all-reduce.3.cloned.1.call-update
  70.2 0.0 all-gather.12.cloned.1.call-start
  70.3 101.9 %all-reduce.3.cloned.1.call-done = (f32[128,1024]{1,0:T(8,128)}, f32[896,1024]{1,0:T(8,128)}) async-done(((f32[128,1024]{1,0:T(8,128)}, f32[896,1024]{1,0:T(8,128)}), (f32[128,1024]{1,0:T(8,128)}, f32[896,1024]{1,0:T(8,128)})) %all-reduce.3.cloned.1.call-update) | async-done | bytes 4194320 | tf_op jit(solution)/shard_map/psum | solution.py:23
  172.2 1.9 broadcast_multiply_fusion.1
  174.1 0.0 all-gather.12.cloned.1.call-update
  174.1 0.0 all-gather.14.cloned.1.call-start
  174.2 46.9 %all-gather.12.cloned.1.call-done = f32[1024,1024]{1,0:T(8,128)} async-done(((f32[128,1024]{1,0:T(8,128)}), f32[1024,1024]{1,0:T(8,128)}) %all-gather.12.cloned.1.call-update) | async-done | bytes 4194320 | tf_op jit(solution)/shard_map/all_gather | solution.py:24
  221.2 17.1 %gather_fusion = f32[1024]{0:T(1024)S(1)} fusion(f32[1024,1024]{1,0:T(8,128)} %all-gather.12.cloned.1.call-done, s32[1024]{0:T(1024)S(1)} %bitcast.16), kind=kCustom, calls=%fused_computation | custom fusion | bytes 16384 | tf_op jit(solution)/shard_map/jit(diagonal)/cond/branch_0_fun/gather | solution.py:26
  238.2 0.6 reduce_sum.18
  239.5 3.9 multiply_reduce_fusion
  244.0 4.7 fusion.16
  248.8 2.5 fusion.28
  251.3 0.0 all-gather.14.cloned.1.call-update
  251.3 0.0 all-gather.16.cloned.1.call-start
  251.3 4.7 fusion.15
  256.0 23.4 %all-gather.14.cloned.1.call-done = bf16[1024,1024]{1,0:T(8,128)(2,1)} async-done(((bf16[128,1024]{1,0:T(8,128)(2,1)}), bf16[1024,1024]{1,0:T(8,128)(2,1)}) %all-gather.14.cloned.1.call-update) | async-done | bytes 2097168 | tf_op jit(solution)/shard_map/all_gather | solution.py:36
  279.4 3.3 fusion.29
  282.7 0.0 all-gather.16.cloned.1.call-update
  282.8 0.2 all-gather.18.cloned.1.call-start
  283.0 4.7 fusion.14
  287.7 23.8 %all-gather.16.cloned.1.call-done = bf16[1024,1024]{1,0:T(8,128)(2,1)} async-done(((bf16[128,1024]{1,0:T(8,128)(2,1)}), bf16[1024,1024]{1,0:T(8,128)(2,1)}) %all-gather.16.cloned.1.call-update) | async-done | bytes 2097168 | tf_op jit(solution)/shard_map/all_gather | solution.py:36
  311.5 3.3 fusion.30
  314.9 0.0 all-gather.18.cloned.1.call-update
  314.9 0.0 all-gather.8.cloned.1.call-start
  314.9 2.3 fusion.17
  317.2 0.0 all-gather.8.cloned.1.call-update
  317.2 0.0 all-gather.20.cloned.1.call-start
  317.3 4.7 fusion.13
  322.0 21.6 %all-gather.18.cloned.1.call-done = bf16[1024,1024]{1,0:T(8,128)(2,1)} async-done(((bf16[128,1024]{1,0:T(8,128)(2,1)}), bf16[1024,1024]{1,0:T(8,128)(2,1)}) %all-gather.18.cloned.1.call-update) | async-done | bytes 2097168 | tf_op jit(solution)/shard_map/all_gather | solution.py:36
  343.6 3.4 convolution_subtract_fusion
  347.0 0.0 all-gather.20.cloned.1.call-update
  347.0 4.6 broadcast_multiply_fusion
  351.6 0.0 copy-start.1
  351.6 40.8 %all-gather.8.cloned.1.call-done = bf16[2048,1024]{1,0:T(8,128)(2,1)} async-done(((bf16[2048,128]{1,0:T(8,128)(2,1)}), bf16[2048,1024]{1,0:T(8,128)(2,1)}) %all-gather.8.cloned.1.call-update) | async-done | bytes 4194320 | tf_op jit(solution)/shard_map/all_gather | solution.py:47
  392.4 46.7 %all-gather.20.cloned.1.call-done = f32[1024,1024]{1,0:T(8,128)} async-done(((f32[128,1024]{1,0:T(8,128)}), f32[1024,1024]{1,0:T(8,128)}) %all-gather.20.cloned.1.call-update) | async-done | bytes 4194320 | tf_op jit(solution)/shard_map/all_gather | solution.py:41
  439.1 16.8 %fusion.32 = f32[2048,1024]{1,0:T(8,128)S(1)} fusion(bf16[2048,1024]{1,0:T(8,128)(2,1)} %all-gather.8.cloned.1.call-done, f32[1024,1024]{1,0:T(8,128)} %all-gather.20.cloned.1.call-done), kind=kOutput, calls=%fused_computation.43 | convolution fusion | flops 25769803776 | bytes 16777216 | tf_op jit(solution)/shard_map/dot_general | solution.py:48
  455.9 0.0 copy-done.1
  455.9 0.0 copy-done
  455.9 0.0 copy-done.2
  455.9 30.5 %multiply_convert_fusion = bf16[2048,1024]{1,0:T(8,128)(2,1)} fusion(bf16[2048,1024]{1,0:T(8,128)(2,1)S(1)} %copy-done.2, s32[2048,1024]{1,0:T(8,128)} %param.5, f32[2048,1024]{1,0:T(8,128)S(1)} %fusion.32, f32[896,1024]{1,0:T(8,128)S(1)} %copy-done, f32[128,1024]{1,0:T(8,128)S(1)} %copy-done.1), kind=kOutput, calls=%fused_computation.1 | convolution fusion | flops 25781338112 | bytes 29360128 | tf_op jit(solution)/shard_map/dot_general | solution.py:49
  (4 shorter events, 0.0 us)
Async XLA Ops:
  6.5 53.0 %all-gather.10.cloned.1.call-start = ((), (), s32[]{:S(2)}) async-start(), calls=%async_computation.1 | async-start | bytes 4718592 | tf_op jit(solution)/shard_map/all_gather | solution.py:19
  8.4 163.8 %all-reduce.3.cloned.1.call-start = ((), (), s32[]{:S(2)}) async-start(), calls=%async_computation.7 | async-start | bytes 8388608 | tf_op jit(solution)/shard_map/psum | solution.py:23
  70.2 150.9 %all-gather.12.cloned.1.call-start = ((), (), s32[]{:S(2)}) async-start(), calls=%async_computation.2 | async-start | bytes 4718592 | tf_op jit(solution)/shard_map/all_gather | solution.py:24
  174.1 105.3 %all-gather.14.cloned.1.call-start = ((), (), s32[]{:S(2)}) async-start(), calls=%async_computation.3 | async-start | bytes 2359296 | tf_op jit(solution)/shard_map/all_gather | solution.py:36
  251.3 60.2 %all-gather.16.cloned.1.call-start = ((), (), s32[]{:S(2)}) async-start(), calls=%async_computation.4 | async-start | bytes 2359296 | tf_op jit(solution)/shard_map/all_gather | solution.py:36
  282.8 60.8 %all-gather.18.cloned.1.call-start = ((), (), s32[]{:S(2)}) async-start(), calls=%async_computation.5 | async-start | bytes 2359296 | tf_op jit(solution)/shard_map/all_gather | solution.py:36
  314.9 77.5 %all-gather.8.cloned.1.call-start = ((), (), s32[]{:S(2)}) async-start(), calls=%async_computation | async-start | bytes 4718592 | tf_op jit(solution)/shard_map/all_gather | solution.py:47
  317.2 121.8 %all-gather.20.cloned.1.call-start = ((), (), s32[]{:S(2)}) async-start(), calls=%async_computation.6 | async-start | bytes 4718592 | tf_op jit(solution)/shard_map/all_gather | solution.py:41
  351.6 104.3 %copy-start.1 = (f32[128,1024]{1,0:T(8,128)S(1)}, f32[128,1024]{1,0:T(8,128)}, u32[]{:S(2)}) copy-start(f32[128,1024]{1,0:T(8,128)} %broadcast_multiply_fusion.1) | copy-start | bytes 1572868
  439.1 16.8 %copy-start = (f32[896,1024]{1,0:T(8,128)S(1)}, f32[896,1024]{1,0:T(8,128)}, u32[]{:S(2)}) copy-start(f32[896,1024]{1,0:T(8,128)} %broadcast_multiply_fusion) | copy-start | bytes 11010052
  439.1 16.8 %copy-start.2 = (bf16[2048,1024]{1,0:T(8,128)(2,1)S(1)}, bf16[2048,1024]{1,0:T(8,128)(2,1)}, u32[]{:S(2)}) copy-start(bf16[2048,1024]{1,0:T(8,128)(2,1)} %param.4) | copy-start | bytes 12582916
Sparse Core Ops, SparseCore 0:
  8.9 50.5 all-gather.9
  70.3 101.8 all-reduce.2
  174.3 46.8 all-gather.11
  251.4 27.9 all-gather.13
  282.9 28.6 all-gather.15
  315.0 28.5 all-gather.17
  345.2 47.2 all-gather.7
  394.0 45.0 all-gather.19
where the time goes:
time: 494 us; the launch traced here: 493 us
  waiting for transfers between devices  356 us (72%)
  matrix products  86.3 us (17%)
  local copies, waits for them, and re-layouts  22.1 us (4%)
  between operations  14.9 us (3%)
  other arithmetic  13.3 us (3%)
    psum x1, waiting for transfers between devices, per_device(): block_part = lax.psum(partial_panel[:panel_width], 'tok') / total_count  102 us
    all_gather x3, waiting for transfers between devices, per_device(): lax.all_gather(iterate.astype(jnp.bfloat16), 'col', axis=0, tiled=True)  68.8 us
    all_gather x1, waiting for transfers between devices, per_device(): lax.all_gather(activations[:, :panel_width], 'col', axis=1, tiled=True)  51 us
    all_gather x1, waiting for transfers between devices, per_device(): diagonal_block = lax.all_gather(block_part, 'col', axis=0, tiled=True)  46.9 us
    all_gather x1, waiting for transfers between devices, per_device(): inverse = lax.all_gather(iterate, 'col', axis=0, tiled=True)  46.7 us
    all_gather x1, waiting for transfers between devices, per_device(): lax.all_gather(pruned, 'col', axis=1, tiled=True).astype(jnp.float32)  40.8 us
    dot_general x1, matrix products, per_device(): lax.dot_general(factor_rows, hessian_panel, (((1,), (1,)), ((), ())), pre...  30.5 us
    dot_general x4, matrix products, per_device(): product = jnp.dot(iterate, damped, precision=highest)  18.8 us
  transfers between devices with their start and end apart: 8, of which 8 were waited for; matrix products, arithmetic and copies ran while one was open for 5% of the time, Pallas kernels for 0%

commit v1 on v0

--- a/solution.py
+++ b/solution.py
@@ -1,3 +1,4 @@
+import functools
 import jax
 import jax.numpy as jnp
 from jax import lax
@@ -5,6 +6,14 @@
 
 B = 1024
 ITERS = 4
+
+
+def assign_shards(m, row_axis):
+    view_out = lax.all_gather(m, axis_name=row_axis)
+    return jnp.sum(view_out, 0)
+
+
+_lift_ladders = functools.partial(assign_shards, row_axis="tok")
 
 
 def per_device(activations, weight, keep_mask):
@@ -20,7 +29,7 @@
         (((0,), (0,)), ((), ())),
         preferred_element_type=jnp.float32,
     )
-    block_part = lax.psum(partial_panel[:panel_width], "tok") / total_count
+    block_part = _lift_ladders(partial_panel[:panel_width]) / total_count
     diagonal_block = lax.all_gather(block_part, "col", axis=0, tiled=True)
     identity = jnp.eye(B, dtype=jnp.float32)
     damping = 0.01 * jnp.mean(jnp.diagonal(diagonal_block))

time: 494 us -> 525 us (1.063)
  waiting for transfers between devices: 356 us -> 382 us
    all_gather x0 -> x1, waiting for transfers between devices: none -> 33.5 us  [assign_shards(): view_out = lax.all_gather(m, axis_name=row_axis)]
    psum x1, waiting for transfers between devices: 102 us -> 94.8 us  [per_device(): remainder = lax.psum(partial_panel[panel_width:], 'tok') / total_count]
  transfers between devices with their start and end apart: 8 -> 9, of which waited for: 8 -> 9; matrix products, arithmetic and copies ran while one was open for 5% -> 6% of each run, Pallas kernels for 0% -> 0%
where the time goes in v1:
time: 525 us; the launch traced here: 524 us
  waiting for transfers between devices  382 us (73%)
  matrix products  86.5 us (16%)
  local copies, waits for them, and re-layouts  25.9 us (5%)
  between operations  14.8 us (3%)
  other arithmetic  14.2 us (3%)
    psum x1, waiting for transfers between devices, per_device(): remainder = lax.psum(partial_panel[panel_width:], 'tok') / total_count  94.8 us
    all_gather x3, waiting for transfers between devices, per_device(): lax.all_gather(iterate.astype(jnp.bfloat16), 'col', axis=0, tiled=True)  64.2 us
    all_gather x1, waiting for transfers between devices, per_device(): lax.all_gather(activations[:, :panel_width], 'col', axis=1, tiled=True)  51 us
    all_gather x1, waiting for transfers between devices, per_device(): diagonal_block = lax.all_gather(block_part, 'col', axis=0, tiled=True)  46.9 us
    all_gather x1, waiting for transfers between devices, per_device(): inverse = lax.all_gather(iterate, 'col', axis=0, tiled=True)  46.7 us
    all_gather x1, waiting for transfers between devices, per_device(): lax.all_gather(pruned, 'col', axis=1, tiled=True).astype(jnp.float32)  44.9 us
    all_gather x1, waiting for transfers between devices, assign_shards(): view_out = lax.all_gather(m, axis_name=row_axis)  33.5 us
    dot_general x1, matrix products, per_device(): lax.dot_general(factor_rows, hessian_panel, (((1,), (1,)), ((), ())), pre...  30.5 us
  transfers between devices with their start and end apart: 9, of which 9 were waited for; matrix products, arithmetic and copies ran while one was open for 6% of the time, Pallas kernels for 0%

profile of v1, /device:TPU:0, one launch (start us, length us, event | category | flops | bytes accessed | tf_op | source)
XLA Modules:
  0.0 523.9 jit_solution(9050981671413676568)
XLA Ops:
  6.5 1.9 slice.17
  8.4 0.0 all-gather.12.cloned.1.call-update
  8.4 0.0 all-gather.24.cloned.1.call-start
  8.5 51.0 %all-gather.12.cloned.1.call-done = bf16[2048,1024]{1,0:T(8,128)(2,1)} async-done(((bf16[2048,128]{1,0:T(8,128)(2,1)}), bf16[2048,1024]{1,0:T(8,128)(2,1)}) %all-gather.12.cloned.1.call-update) | async-done | bytes 4194320 | tf_op jit(solution)/shard_map/all_gather | solution.py:28
  59.5 7.6 %fusion.31 = f32[1024,1024]{1,0:T(8,128)S(1)} fusion(bf16[2048,1024]{1,0:T(8,128)(2,1)} %param.3, bf16[2048,1024]{1,0:T(8,128)(2,1)} %all-gather.12.cloned.1.call-done), kind=kOutput, calls=%fused_computation.42 | convolution fusion | flops 4294967296 | bytes 12582912 | tf_op jit(solution)/shard_map/dot_general | solution.py:26
  67.1 2.0 copy-done
  69.1 0.8 slice.22
  69.9 0.0 all-gather.24.cloned.1.call-update
  70.0 0.0 all-gather.14.cloned.1.call-start
  70.0 33.5 %all-gather.24.cloned.1.call-done = f32[512,1024]{1,0:T(8,128)} async-done(((f32[128,1024]{1,0:T(8,128)}), f32[512,1024]{1,0:T(8,128)}) %all-gather.24.cloned.1.call-update) | async-done | bytes 2097168 | tf_op jit(solution)/shard_map/all_gather | solution.py:12
  103.5 1.8 reduce_sum.27
  105.3 0.8 broadcast_multiply_fusion.1
  106.1 0.0 all-gather.14.cloned.1.call-update
  106.1 0.0 all-gather.16.cloned.1.call-start
  106.2 46.9 %all-gather.14.cloned.1.call-done = f32[1024,1024]{1,0:T(8,128)} async-done(((f32[128,1024]{1,0:T(8,128)}), f32[1024,1024]{1,0:T(8,128)}) %all-gather.14.cloned.1.call-update) | async-done | bytes 4194320 | tf_op jit(solution)/shard_map/all_gather | solution.py:33
  153.2 16.8 %gather_fusion = f32[1024]{0:T(1024)S(1)} fusion(f32[1024,1024]{1,0:T(8,128)} %all-gather.14.cloned.1.call-done, s32[1024]{0:T(1024)S(1)} %bitcast.17), kind=kCustom, calls=%fused_computation | custom fusion | bytes 16384 | tf_op jit(solution)/shard_map/jit(diagonal)/cond/branch_0_fun/gather | solution.py:35
  170.0 0.7 reduce_sum.28
  171.4 4.0 multiply_reduce_fusion
  176.1 4.7 fusion.16
  180.8 2.5 fusion.28
  183.3 0.0 all-gather.16.cloned.1.call-update
  183.4 0.0 all-gather.18.cloned.1.call-start
  183.4 4.7 fusion.15
  188.1 23.4 %all-gather.16.cloned.1.call-done = bf16[1024,1024]{1,0:T(8,128)(2,1)} async-done(((bf16[128,1024]{1,0:T(8,128)(2,1)}), bf16[1024,1024]{1,0:T(8,128)(2,1)}) %all-gather.16.cloned.1.call-update) | async-done | bytes 2097168 | tf_op jit(solution)/shard_map/all_gather | solution.py:45
  211.5 3.3 fusion.29
  214.8 0.0 all-gather.18.cloned.1.call-update
  214.8 0.2 all-gather.20.cloned.1.call-start
  215.1 4.7 fusion.14
  219.8 23.8 %all-gather.18.cloned.1.call-done = bf16[1024,1024]{1,0:T(8,128)(2,1)} async-done(((bf16[128,1024]{1,0:T(8,128)(2,1)}), bf16[1024,1024]{1,0:T(8,128)(2,1)}) %all-gather.18.cloned.1.call-update) | async-done | bytes 2097168 | tf_op jit(solution)/shard_map/all_gather | solution.py:45
  243.6 3.3 fusion.30
  247.0 0.0 all-gather.20.cloned.1.call-update
  247.0 0.0 all-reduce.2.cloned.1.call-start
  247.0 4.4 slice.23
  251.4 0.0 all-reduce.2.cloned.1.call-update
  251.4 0.0 all-gather.10.cloned.1.call-start
  251.5 2.3 fusion.17
  253.8 0.0 all-gather.10.cloned.1.call-update
  253.8 0.0 all-gather.22.cloned.1.call-start
  253.9 4.9 fusion.13
  258.7 16.9 %all-gather.20.cloned.1.call-done = bf16[1024,1024]{1,0:T(8,128)(2,1)} async-done(((bf16[128,1024]{1,0:T(8,128)(2,1)}), bf16[1024,1024]{1,0:T(8,128)(2,1)}) %all-gather.20.cloned.1.call-update) | async-done | bytes 2097168 | tf_op jit(solution)/shard_map/all_gather | solution.py:45
  275.7 3.4 convolution_subtract_fusion
  279.1 0.0 all-gather.22.cloned.1.call-update
  279.1 94.8 %all-reduce.2.cloned.1.call-done = f32[896,1024]{1,0:T(8,128)} async-done(((f32[896,1024]{1,0:T(8,128)}), f32[896,1024]{1,0:T(8,128)}) %all-reduce.2.cloned.1.call-update) | async-done | bytes 3670032 | tf_op jit(solution)/shard_map/psum | solution.py:51
  373.9 4.6 broadcast_multiply_fusion
  378.5 44.9 %all-gather.10.cloned.1.call-done = bf16[2048,1024]{1,0:T(8,128)(2,1)} async-done(((bf16[2048,128]{1,0:T(8,128)(2,1)}), bf16[2048,1024]{1,0:T(8,128)(2,1)}) %all-gather.10.cloned.1.call-update) | async-done | bytes 4194320 | tf_op jit(solution)/shard_map/all_gather | solution.py:56
  423.3 46.7 %all-gather.22.cloned.1.call-done = f32[1024,1024]{1,0:T(8,128)} async-done(((f32[128,1024]{1,0:T(8,128)}), f32[1024,1024]{1,0:T(8,128)}) %all-gather.22.cloned.1.call-update) | async-done | bytes 4194320 | tf_op jit(solution)/shard_map/all_gather | solution.py:50
  470.0 16.8 %fusion.32 = f32[2048,1024]{1,0:T(8,128)S(1)} fusion(bf16[2048,1024]{1,0:T(8,128)(2,1)} %all-gather.10.cloned.1.call-done, f32[1024,1024]{1,0:T(8,128)} %all-gather.22.cloned.1.call-done), kind=kOutput, calls=%fused_computation.43 | convolution fusion | flops 25769803776 | bytes 16777216 | tf_op jit(solution)/shard_map/dot_general | solution.py:57
  486.9 30.5 %multiply_convert_fusion = bf16[2048,1024]{1,0:T(8,128)(2,1)} fusion(bf16[2048,1024]{1,0:T(8,128)(2,1)S(1)} %copy-done.3, s32[2048,1024]{1,0:T(8,128)} %param.5, f32[2048,1024]{1,0:T(8,128)S(1)} %fusion.32, f32[896,1024]{1,0:T(8,128)S(1)} %copy-done.1, f32[128,1024]{1,0:T(8,128)S(1)} %copy-done.2), kind=kOutput, calls=%fused_computation.1 | convolution fusion | flops 25781338112 | bytes 29360128 | tf_op jit(solution)/shard_map/dot_general | solution.py:58
  (10 shorter events, 0.0 us)
Async XLA Ops:
  6.5 53.0 %all-gather.12.cloned.1.call-start = ((), (), s32[]{:S(2)}) async-start(), calls=%async_computation.1 | async-start | bytes 4718592 | tf_op jit(solution)/shard_map/all_gather | solution.py:28
  8.4 95.0 %all-gather.24.cloned.1.call-start = ((), (), s32[]{:S(2)}) async-start(), calls=%async_computation.8 | async-start | bytes 2621440 | tf_op jit(solution)/shard_map/all_gather | solution.py:12
  67.1 2.0 copy-start
  70.0 83.2 %all-gather.14.cloned.1.call-start = ((), (), s32[]{:S(2)}) async-start(), calls=%async_computation.2 | async-start | bytes 4718592 | tf_op jit(solution)/shard_map/all_gather | solution.py:33
  106.1 105.3 %all-gather.16.cloned.1.call-start = ((), (), s32[]{:S(2)}) async-start(), calls=%async_computation.3 | async-start | bytes 2359296 | tf_op jit(solution)/shard_map/all_gather | solution.py:45
  183.4 60.3 %all-gather.18.cloned.1.call-start = ((), (), s32[]{:S(2)}) async-start(), calls=%async_computation.4 | async-start | bytes 2359296 | tf_op jit(solution)/shard_map/all_gather | solution.py:45
  214.8 60.8 %all-gather.20.cloned.1.call-start = ((), (), s32[]{:S(2)}) async-start(), calls=%async_computation.5 | async-start | bytes 2359296 | tf_op jit(solution)/shard_map/all_gather | solution.py:45
  247.0 126.9 %all-reduce.2.cloned.1.call-start = ((), (), s32[]{:S(2)}) async-start(), calls=%async_computation.7 | async-start | bytes 7340032 | tf_op jit(solution)/shard_map/psum | solution.py:51
  251.4 171.9 %all-gather.10.cloned.1.call-start = ((), (), s32[]{:S(2)}) async-start(), calls=%async_computation | async-start | bytes 4718592 | tf_op jit(solution)/shard_map/all_gather | solution.py:56
  253.8 216.2 %all-gather.22.cloned.1.call-start = ((), (), s32[]{:S(2)}) async-start(), calls=%async_computation.6 | async-start | bytes 4718592 | tf_op jit(solution)/shard_map/all_gather | solution.py:50
  378.5 108.3 %copy-start.2 = (f32[128,1024]{1,0:T(8,128)S(1)}, f32[128,1024]{1,0:T(8,128)}, u32[]{:S(2)}) copy-start(f32[128,1024]{1,0:T(8,128)} %broadcast_multiply_fusion.1) | copy-start | bytes 1572868
  470.0 16.8 %copy-start.1 = (f32[896,1024]{1,0:T(8,128)S(1)}, f32[896,1024]{1,0:T(8,128)}, u32[]{:S(2)}) copy-start(f32[896,1024]{1,0:T(8,128)} %broadcast_multiply_fusion) | copy-start | bytes 11010052
  470.0 16.8 %copy-start.3 = (bf16[2048,1024]{1,0:T(8,128)(2,1)S(1)}, bf16[2048,1024]{1,0:T(8,128)(2,1)}, u32[]{:S(2)}) copy-start(bf16[2048,1024]{1,0:T(8,128)(2,1)} %param.4) | copy-start | bytes 12582916
Sparse Core Ops, SparseCore 0:
  8.9 50.5 all-gather.11
  70.1 33.3 all-gather.23
  106.3 46.8 all-gather.13
  183.5 27.9 all-gather.15
  215.0 28.6 all-gather.17
  247.1 28.5 all-gather.19
  278.8 95.0 all-reduce.1
  375.5 47.8 all-gather.9
  424.9 45.0 all-gather.21
